TPU v7x, 32 devices: a whole 2x2x4 slice. The times are simulated.
32 devices in a mesh: mp: 2 (over y), fsdp: 8 (over z, core), tp: 2 (over x).
Axes of the slice: x: 2, y: 2, z: 4, core: 2. Of those that a mesh axis runs over, the one named last changes fastest.
Arguments:
- hidden: bfloat16 [2, 1280, 5120], P('mp', 'fsdp'), may hold values from -6 to 6
- live_weight: bfloat16 [2, 5120, 1024], P('mp', 'fsdp', 'tp'), may hold values from -0.078125 to 0.078125
- stale_weight: bfloat16 [2, 5120, 1024], P('mp', 'fsdp', 'tp'), may hold values from -0.078125 to 0.078125
- match: int32 [2, 1280], P('mp', 'fsdp'), may hold values from 0 to 159, as said below
Outputs:
- hidden_grad: bfloat16 [2, 1280, 5120], P('mp', 'fsdp', 'tp')
Inputs may be any that keep to these rules, and one draw needn't show every extreme that they name: Within each model's block of 160 rows, match is a permutation of 0 to 159, and the two models' permutations of a block are inverse to each other.
All inputs are finite; a program needn't handle non-finite values.
Results may differ from a plain program's by a relative error of at most 0.0061.
Values may be sent and summed in bfloat16 or wider, within the bound.
No kernel may reach another device: no remote copies, remote signals or barrier semaphores. Data moves between devices by JAX's collectives and lax.ppermute only.
A program may use at most 64 MiB of HBM per device.

v0:
```python
import jax
import jax.numpy as jnp
from jax import lax
from jax.sharding import PartitionSpec as P


def partner(block, axis, apart):
    count = lax.axis_size(axis)
    route = []
    for low in range(count):
        high = low | 1 << apart
        if high != low and high < count:
            route += [(low, high), (high, low)]
    return lax.ppermute(block, axis, route)


def shards(hidden, live_weight, stale_weight, match):
    hidden_rows = hidden[0]
    live_full = lax.all_gather(live_weight[0], "fsdp", axis=0, tiled=True)
    student = jnp.dot(hidden_rows, live_full, preferred_element_type=jnp.float32)
    stale_piece = stale_weight[0]
    teacher = jnp.dot(
        hidden_rows,
        lax.all_gather(stale_piece, "fsdp", axis=0, tiled=True),
        preferred_element_type=jnp.float32,
    ).astype(jnp.bfloat16)
    teacher = partner(teacher, "mp", 0)
    target = jnp.take(teacher, match[0], axis=0)
    mismatch = (student - target.astype(jnp.float32)).astype(jnp.bfloat16)
    partial_value = lax.dot_general(
        mismatch, live_full, (((1,), (1,)), ((), ())), preferred_element_type=jnp.float32
    )
    summed = lax.psum_scatter(
        partial_value.astype(jnp.bfloat16), "tp", scatter_dimension=1, tiled=True
    )
    return summed[None]


def solution(mesh):
    in_specs = (
        P("mp", "fsdp", None),
        P("mp", "fsdp", "tp"),
        P("mp", "fsdp", "tp"),
        P("mp", "fsdp"),
    )
    out_specs = P("mp", "fsdp", "tp")
    return jax.shard_map(shards, mesh=mesh, in_specs=in_specs, out_specs=out_specs, check_vma=False)
```

profile of v0, /device:TPU:0, one launch (start us, length us, event | category | flops | bytes accessed | tf_op | source)
XLA Modules:
  0.0 164.6 jit_solution(195391604350372213)
XLA Ops:
  6.5 0.0 copy-start
  6.5 0.0 copy-start.1
  6.5 0.0 all-gather.7.cloned.1.call-start
  6.5 0.7 all-gather.7.cloned.1.call-update
  7.3 0.0 all-gather.5.cloned.1.call-start
  7.3 0.7 all-gather.5.cloned.1.call-update
  8.0 0.0 reduce-scatter.2.cloned.1.call-start
  8.1 0.7 compare_select_fusion
  8.7 59.0 %all-gather.7.cloned.1.call-done = bf16[1,5120,512]{2,1,0:T(8,128)(2,1)} async-done(((bf16[1,640,512]{2,1,0:T(8,128)(2,1)}), bf16[1,5120,512]{2,1,0:T(8,128)(2,1)}) %all-gather.7.cloned.1.call-update) | async-done | bytes 5242896 | tf_op jit(solution)/shard_map/all_gather | solution.py:24
  67.8 0.0 copy-done
  67.8 3.5 %fusion.7 = bf16[160,512]{1,0:T(8,128)(2,1)S(1)} fusion(bf16[1,5120,512]{2,1,0:T(8,128)(2,1)} %all-gather.7.cloned.1.call-done, bf16[1,160,5120]{2,1,0:T(8,128)(2,1)S(1)} %copy-done), kind=kOutput, calls=%fused_computation.9 | convolution fusion | flops 838942720 | bytes 7045120 | tf_op jit(solution)/shard_map/dot_general | solution.py:22
  71.3 1.5 collective-permute-start
  72.8 0.0 copy-done.1
  72.9 4.8 %collective-permute-done = bf16[160,512]{1,0:T(8,128)(2,1)S(1)} collective-permute-done((bf16[160,512]{1,0:T(8,128)(2,1)S(1)}, bf16[160,512]{1,0:T(8,128)(2,1)S(1)}, u32[]{:S(2)}, u32[]{:S(2)}) %collective-permute-start) | collective-permute-done | bytes 163872 | tf_op jit(solution)/shard_map/ppermute | solution.py:14
  77.7 0.9 gather_fusion
  78.6 45.6 %all-gather.5.cloned.1.call-done = bf16[1,5120,512]{2,1,0:T(8,128)(2,1)} async-done(((bf16[1,640,512]{2,1,0:T(8,128)(2,1)}), bf16[1,5120,512]{2,1,0:T(8,128)(2,1)}) %all-gather.5.cloned.1.call-update) | async-done | bytes 5242896 | tf_op jit(solution)/shard_map/all_gather | solution.py:19
  124.3 8.1 %convolution_convert_fusion = bf16[160,5120]{1,0:T(8,128)(2,1)} fusion(bf16[1,5120,512]{2,1,0:T(8,128)(2,1)} %all-gather.5.cloned.1.call-done, bf16[1,160,5120]{2,1,0:T(8,128)(2,1)S(1)} %copy-done, bf16[160,512]{1,0:T(8,128)(2,1)S(1)} %gather_fusion, pred[160]{0:T(512)(128)(4,1)S(1)} %compare_and_fusion), kind=kOutput, calls=%fused_computation.1 | convolution fusion | flops 1678868480 | bytes 8683680 | tf_op jit(solution)/shard_map/dot_general | solution.py:30
  132.3 0.0 reduce-scatter.2.cloned.1.call-update
  132.4 25.7 %reduce-scatter.2.cloned.1.call-done = bf16[160,2560]{1,0:T(8,128)(2,1)} async-done(((bf16[160,5120]{1,0:T(8,128)(2,1)}), bf16[160,2560]{1,0:T(8,128)(2,1)}) %reduce-scatter.2.cloned.1.call-update) | async-done | bytes 819216 | tf_op jit(solution)/shard_map/reduce_scatter | solution.py:33
  (2 shorter events, 0.0 us)
Async XLA Ops:
  6.5 61.2 %copy-start = (bf16[1,160,5120]{2,1,0:T(8,128)(2,1)S(1)}, bf16[1,160,5120]{2,1,0:T(8,128)(2,1)}, u32[]{:S(2)}) copy-start(bf16[1,160,5120]{2,1,0:T(8,128)(2,1)} %param.4) | copy-start | bytes 4915204
  6.5 66.3 %copy-start.1 = (s32[1,160]{1,0:T(1,128)S(1)}, s32[1,160]{1,0:T(1,128)}, u32[]{:S(2)}) copy-start(s32[1,160]{1,0:T(1,128)} %param.7) | copy-start | bytes 1924
  6.5 61.2 %all-gather.7.cloned.1.call-start = ((), (), s32[]{:S(2)}) async-start(), calls=%async_computation.3 | async-start | bytes 5898240 | tf_op jit(solution)/shard_map/all_gather | solution.py:24
  7.3 117.0 %all-gather.5.cloned.1.call-start = ((), (), s32[]{:S(2)}) async-start(), calls=%async_computation.2 | async-start | bytes 5898240 | tf_op jit(solution)/shard_map/all_gather | solution.py:19
  8.0 150.1 %reduce-scatter.2.cloned.1.call-start = ((), (), s32[]{:S(2)}) async-start(), calls=%async_computation.1 | async-start | bytes 2457600 | tf_op jit(solution)/shard_map/reduce_scatter | solution.py:33
  71.3 6.4 %collective-permute-start = (bf16[160,512]{1,0:T(8,128)(2,1)S(1)}, bf16[160,512]{1,0:T(8,128)(2,1)S(1)}, u32[]{:S(2)}, u32[]{:S(2)}) collective-permute-start(bf16[160,512]{1,0:T(8,128)(2,1)S(1)} %fusion.7), channel_id=1, source_target_pairs={{0,16},{16,0},{1,17},{17,1},{2,18},{18,2},{3,19},{19,3},{4,20},{20... | collective-permute-start | bytes 491528 | tf_op jit(solution)/shard_map/ppermute | solution.py:14
Sparse Core Ops, SparseCore 0:
  9.0 58.7 all-gather.6
  69.4 54.8 all-gather.4
  132.5 25.5 reduce-scatter.1
where the time goes:
time: 165 us
  waiting for transfers between devices  137 us (83%)
  between operations  13.1 us (8%)
  matrix products  11.6 us (7%)
    all_gather x1, waiting for transfers between devices, shards(): lax.all_gather(stale_piece, 'fsdp', axis=0, tiled=True)  59 us
    all_gather x1, waiting for transfers between devices, shards(): live_full = lax.all_gather(live_weight[0], 'fsdp', axis=0, tiled=True)  45.6 us
    reduce_scatter x1, waiting for transfers between devices, shards(): lax.psum_scatter(partial_value.astype(jnp.bfloat16), 'tp', scatter_dimens...  25.7 us
    dot_general x1, matrix products, shards(): lax.dot_general(mismatch, live_full, (((1,), (1,)), ((), ())), preferred_...  8.07 us
    ppermute x1, waiting for transfers between devices, partner(): return lax.ppermute(block, axis, route)  4.84 us
    dot_general x1, matrix products, shards(): jnp.dot(hidden_rows, lax.all_gather(stale_piece, 'fsdp', axis=0, tiled=Tr...  3.5 us
  transfers between devices with their start and end apart: 4, of which 4 were waited for; matrix products, arithmetic and copies ran while one was open for 3% of the time, Pallas kernels for 0%

commit v1 on v0

--- a/solution.py
+++ b/solution.py
@@ -2,6 +2,29 @@
 import jax.numpy as jnp
 from jax import lax
 from jax.sharding import PartitionSpec as P
+
+
+def column_track(payload, k_dim):
+    clean = list(payload.shape[1:])
+    clean[k_dim] *= payload.shape[0]
+    e_next = jnp.moveaxis(payload, 0, k_dim).reshape(clean)
+    return e_next
+
+
+def arrange_pipes(mine_x, along_axis):
+    arr_out, ready = (lax.axis_size(along_axis), lax.axis_index(along_axis))
+    z_new, passed = (mine_x[None], 1)
+    while passed < arr_out:
+        spare = lax.ppermute(z_new, along_axis, tuple(((d, d ^ passed) for d in range(arr_out))))
+        y = ready & passed == 0
+        z_new = jnp.concatenate([jnp.where(y, z_new, spare), jnp.where(y, spare, z_new)])
+        passed *= 2
+    return z_new
+
+
+def numbers_note(matrix, local_block, at_axis):
+    later = column_track(arrange_pipes(matrix, local_block), at_axis)
+    return later
 
 
 def partner(block, axis, apart):
@@ -20,9 +43,7 @@
     student = jnp.dot(hidden_rows, live_full, preferred_element_type=jnp.float32)
     stale_piece = stale_weight[0]
     teacher = jnp.dot(
-        hidden_rows,
-        lax.all_gather(stale_piece, "fsdp", axis=0, tiled=True),
-        preferred_element_type=jnp.float32,
+        hidden_rows, numbers_note(stale_piece, "fsdp", 0), preferred_element_type=jnp.float32
     ).astype(jnp.bfloat16)
     teacher = partner(teacher, "mp", 0)
     target = jnp.take(teacher, match[0], axis=0)

time: 165 us -> 259 us (1.57)
  waiting for transfers between devices: 137 us -> 220 us
  other arithmetic: 0.7 us -> 7.82 us
  starting transfers between devices: 1.62 us -> 6.62 us
    ppermute x0 -> x3, waiting for transfers between devices: none -> 187 us  [arrange_pipes(): lax.ppermute(z_new, along_axis, tuple(((d, d ^ passed) for d in range(arr...]
    all_gather x1 -> x0, waiting for transfers between devices: 59 us -> none  [shards(): lax.all_gather(stale_piece, 'fsdp', axis=0, tiled=True)]
    all_gather x1, waiting for transfers between devices: 45.6 us -> 0.02 us  [shards(): live_full = lax.all_gather(live_weight[0], 'fsdp', axis=0, tiled=True)]
    select_n x0 -> x3, other arithmetic: none -> 5.29 us  [arrange_pipes(): jnp.where(y, z_new, spare)]
    ppermute x0 -> x3, starting transfers between devices: none -> 5.21 us  [arrange_pipes(): lax.ppermute(z_new, along_axis, tuple(((d, d ^ passed) for d in range(arr...]
  transfers between devices with their start and end apart: 4 -> 6, of which waited for: 4 -> 5; matrix products, arithmetic and copies ran while one was open for 3% -> 4% of each run, Pallas kernels for 0% -> 0%
where the time goes in v1:
time: 259 us
  waiting for transfers between devices  220 us (85%)
  between operations  13.5 us (5%)
  matrix products  9.06 us (3%)
  other arithmetic  7.82 us (3%)
  starting transfers between devices  6.62 us (3%)
    ppermute x3, waiting for transfers between devices, arrange_pipes(): lax.ppermute(z_new, along_axis, tuple(((d, d ^ passed) for d in range(arr...  187 us
    reduce_scatter x1, waiting for transfers between devices, shards(): lax.psum_scatter(partial_value.astype(jnp.bfloat16), 'tp', scatter_dimens...  27.7 us
    dot_general x1, matrix products, shards(): lax.dot_general(mismatch, live_full, (((1,), (1,)), ((), ())), preferred_...  8.05 us
    select_n x3, other arithmetic, arrange_pipes(): jnp.where(y, z_new, spare)  5.29 us
    ppermute x3, starting transfers between devices, arrange_pipes(): lax.ppermute(z_new, along_axis, tuple(((d, d ^ passed) for d in range(arr...  5.21 us
  transfers between devices with their start and end apart: 6, of which 5 were waited for; matrix products, arithmetic and copies ran while one was open for 4% of the time, Pallas kernels for 0%

profile of v1, /device:TPU:0, one launch (start us, length us, event | category | flops | bytes accessed | tf_op | source)
XLA Modules:
  0.0 258.6 jit_solution(16023624325789030812)
XLA Ops:
  6.5 0.7 all-gather.3.cloned.1.call-update
  7.3 0.0 reduce-scatter.2.cloned.1.call-start
  7.3 0.5 collective-permute-start
  7.8 1.9 collective-permute-done
  9.8 1.2 broadcast_select_fusion.5
  11.0 0.8 copy-done.2
  11.8 0.1 pad_maximum_fusion.2
  11.9 0.1 copy-done.3
  12.0 2.9 %collective-permute-start.1 = (bf16[2,640,512]{2,1,0:T(8,128)(2,1)S(1)}, bf16[2,640,512]{2,1,0:T(8,128)(2,1)}, u32[]{:S(2)}, u32[]{:S(2)}) collective-permute-start(bf16[2,640,512]{2,1,0:T(8,128)(2,1)S(1)} %pad_maximum_fusion.2), channel_id=1, source_target_pairs={{0,4},{2,6},{4,0},{6,2},{8,12},{10,14},{12,8},{14,10},{1,5},{3,7},... | collective-permute-start | bytes 3932168 | tf_op jit(solution)/shard_map/ppermute | solution.py:18
  14.9 71.3 %collective-permute-done.1 = bf16[2,640,512]{2,1,0:T(8,128)(2,1)} collective-permute-done((bf16[2,640,512]{2,1,0:T(8,128)(2,1)S(1)}, bf16[2,640,512]{2,1,0:T(8,128)(2,1)}, u32[]{:S(2)}, u32[]{:S(2)}) %collective-permute-start.1) | collective-permute-done | bytes 1310752 | tf_op jit(solution)/shard_map/ppermute | solution.py:18
  86.2 1.9 broadcast_select_fusion.3
  88.1 1.9 pad_maximum_fusion.1
  90.1 1.7 collective-permute-start.2
  91.8 114.1 %collective-permute-done.2 = bf16[4,640,512]{2,1,0:T(8,128)(2,1)} collective-permute-done((bf16[4,640,512]{2,1,0:T(8,128)(2,1)}, bf16[4,640,512]{2,1,0:T(8,128)(2,1)}, u32[]{:S(2)}, u32[]{:S(2)}) %collective-permute-start.2) | collective-permute-done | bytes 2621472 | tf_op jit(solution)/shard_map/ppermute | solution.py:18
  205.9 2.3 broadcast_select_fusion.1
  208.2 0.5 pad_maximum_fusion
  208.7 1.0 fusion.9
  209.7 1.4 collective-permute-start.3
  211.1 4.0 %collective-permute-done.3 = bf16[160,512]{1,0:T(8,128)(2,1)S(1)} collective-permute-done((bf16[160,512]{1,0:T(8,128)(2,1)S(1)}, bf16[160,512]{1,0:T(8,128)(2,1)S(1)}, u32[]{:S(2)}, u32[]{:S(2)}) %collective-permute-start.3) | collective-permute-done | bytes 163872 | tf_op jit(solution)/shard_map/ppermute | solution.py:37
  215.1 0.9 gather_fusion
  216.0 0.0 all-gather.3.cloned.1.call-done
  216.0 8.1 %convolution_convert_fusion = bf16[160,5120]{1,0:T(8,128)(2,1)} fusion(bf16[1,5120,512]{2,1,0:T(8,128)(2,1)} %all-gather.3.cloned.1.call-done, bf16[1,160,5120]{2,1,0:T(8,128)(2,1)S(1)} %copy-done, bf16[160,512]{1,0:T(8,128)(2,1)S(1)} %gather_fusion, pred[160]{0:T(512)(128)(4,1)S(1)} %compare_and_fusion), kind=kOutput, calls=%fused_computation.1 | convolution fusion | flops 1678868480 | bytes 8683680 | tf_op jit(solution)/shard_map/dot_general | solution.py:51
  224.1 0.0 reduce-scatter.2.cloned.1.call-update
  224.1 27.7 %reduce-scatter.2.cloned.1.call-done = bf16[160,2560]{1,0:T(8,128)(2,1)} async-done(((bf16[160,5120]{1,0:T(8,128)(2,1)}), bf16[160,2560]{1,0:T(8,128)(2,1)}) %reduce-scatter.2.cloned.1.call-update) | async-done | bytes 819216 | tf_op jit(solution)/shard_map/reduce_scatter | solution.py:54
  (12 shorter events, 0.0 us)
Async XLA Ops:
  6.5 202.1 %copy-start = (bf16[1,160,5120]{2,1,0:T(8,128)(2,1)S(1)}, bf16[1,160,5120]{2,1,0:T(8,128)(2,1)}, u32[]{:S(2)}) copy-start(bf16[1,160,5120]{2,1,0:T(8,128)(2,1)} %param.4) | copy-start | bytes 4915204
  6.5 209.5 %all-gather.3.cloned.1.call-start = ((), (), s32[]{:S(2)}) async-start(), calls=%async_computation.2 | async-start | bytes 5898240 | tf_op jit(solution)/shard_map/all_gather | solution.py:42
  7.3 244.5 %reduce-scatter.2.cloned.1.call-start = ((), (), s32[]{:S(2)}) async-start(), calls=%async_computation.1 | async-start | bytes 2457600 | tf_op jit(solution)/shard_map/reduce_scatter | solution.py:54
  7.3 2.5 collective-permute-start
  10.9 0.8 copy-start.2
  10.9 1.0 copy-start.3
  12.0 74.3 %collective-permute-start.1 = (bf16[2,640,512]{2,1,0:T(8,128)(2,1)S(1)}, bf16[2,640,512]{2,1,0:T(8,128)(2,1)}, u32[]{:S(2)}, u32[]{:S(2)}) collective-permute-start(bf16[2,640,512]{2,1,0:T(8,128)(2,1)S(1)} %pad_maximum_fusion.2), channel_id=1, source_target_pairs={{0,4},{2,6},{4,0},{6,2},{8,12},{10,14},{12,8},{14,10},{1,5},{3,7},... | collective-permute-start | bytes 3932168 | tf_op jit(solution)/shard_map/ppermute | solution.py:18
  88.1 2.0 copy-start.1
  88.1 3.7 %copy-start.4 = (s32[1,160]{1,0:T(1,128)S(1)}, s32[1,160]{1,0:T(1,128)}, u32[]{:S(2)}) copy-start(s32[1,160]{1,0:T(1,128)} %param.7) | copy-start | bytes 1924
  90.1 115.8 %collective-permute-start.2 = (bf16[4,640,512]{2,1,0:T(8,128)(2,1)}, bf16[4,640,512]{2,1,0:T(8,128)(2,1)}, u32[]{:S(2)}, u32[]{:S(2)}) collective-permute-start(bf16[4,640,512]{2,1,0:T(8,128)(2,1)} %pad_maximum_fusion.1), channel_id=1, source_target_pairs={{0,8},{2,10},{4,12},{6,14},{8,0},{10,2},{12,4},{14,6},{1,9},{3,11}... | collective-permute-start | bytes 7864328 | tf_op jit(solution)/shard_map/ppermute | solution.py:18
  209.7 5.4 %collective-permute-start.3 = (bf16[160,512]{1,0:T(8,128)(2,1)S(1)}, bf16[160,512]{1,0:T(8,128)(2,1)S(1)}, u32[]{:S(2)}, u32[]{:S(2)}) collective-permute-start(bf16[160,512]{1,0:T(8,128)(2,1)S(1)} %fusion.9), channel_id=1, source_target_pairs={{0,16},{16,0},{1,17},{17,1},{2,18},{18,2},{3,19},{19,3},{4,20},{20... | collective-permute-start | bytes 491528 | tf_op jit(solution)/shard_map/ppermute | solution.py:37
Sparse Core Ops, SparseCore 0:
  9.0 78.2 all-gather.2
  224.2 27.5 reduce-scatter.1
